TPU v7x, 32 devices: a whole 2x2x4 slice. The times are simulated.
32 devices in a mesh: dp: 8 (over y, x, core), tensor: 4 (over z).
Axes of the slice: x: 2, y: 2, z: 4, core: 2. Of those that a mesh axis runs over, the one named last changes fastest.
Arguments:
- latents: bfloat16 [16384, 1280], P('dp'), may hold values from -6 to 6
- norm1_gain: float32 [1280], replicated, may hold values from 0.5 to 1.5
- norm1_shift: float32 [1280], replicated, may hold values from -1.75 to 1.75
- query_weight: bfloat16 [1280, 1280], P(None, 'tensor'), may hold values from -0.15625 to 0.15625
- query_bias: float32 [1280], P('tensor'), may hold values from -1.75 to 1.75
- key_weight: bfloat16 [1280, 1280], P(None, 'tensor'), may hold values from -0.15625 to 0.15625
- value_weight: bfloat16 [1280, 1280], P(None, 'tensor'), may hold values from -0.15625 to 0.15625
- value_bias: float32 [1280], P('tensor'), may hold values from -1.75 to 1.75
- out_weight: bfloat16 [1280, 1280], P('tensor'), may hold values from -0.625 to 0.625
- out_bias: float32 [1280], replicated, may hold values from -1.75 to 1.75
- norm2_gain: float32 [1280], replicated, may hold values from 0.5 to 1.5
- norm2_shift: float32 [1280], replicated, may hold values from -1.75 to 1.75
- hidden_weight: bfloat16 [1280, 1280], P(None, 'tensor'), may hold values from -0.15625 to 0.15625
- hidden_bias: float32 [1280], P('tensor'), may hold values from -1.75 to 1.75
- proj_weight: bfloat16 [1280, 1280], P('tensor'), may hold values from -0.25 to 0.25
- proj_bias: float32 [1280], replicated, may hold values from -1.75 to 1.75
- segments: int32 [16, 1024], P('dp'), may hold values from 0 to 7, never falling along the last dimension, each value on 1 to 512 neighbouring positions
- valid_mask: int32 [16, 1024], P('dp'), may hold values 0 or 1
- cotangent: bfloat16 [16384, 1280], P('dp'), may hold values from -6 to 6
Outputs:
- output: bfloat16 [16384, 1280], P('dp')
- grad_input: float32 [16384, 1280], P('dp')
- grad_norm1_gain: float32 [1280], replicated
- grad_norm1_shift: float32 [1280], replicated
- grad_query_weight: float32 [1280, 1280], P(None, 'tensor')
- grad_query_bias: float32 [1280], P('tensor')
- grad_key_weight: float32 [1280, 1280], P(None, 'tensor')
- grad_value_weight: float32 [1280, 1280], P(None, 'tensor')
- grad_value_bias: float32 [1280], P('tensor')
- grad_out_weight: float32 [1280, 1280], P('tensor')
- grad_out_bias: float32 [1280], replicated
- grad_norm2_gain: float32 [1280], replicated
- grad_norm2_shift: float32 [1280], replicated
- grad_hidden_weight: float32 [1280, 1280], P(None, 'tensor')
- grad_hidden_bias: float32 [1280], P('tensor')
- grad_proj_weight: float32 [1280, 1280], P('tensor')
- grad_proj_bias: float32 [1280], replicated
- rms: float32 [16, 3], P('dp')
Inputs may be any that keep to these rules, and one draw needn't show every extreme that they name: `segments`: in each row segment numbers never fall, each document has 1 to 512 positions, and one has exactly that many.
All inputs are finite; a program needn't handle non-finite values. No bound on the sum of `valid_mask` on one device may be relied on, other than what follows from the above.
Results may differ from a plain program's by a relative error of at most 0.013.
Values sent between devices are 32-bit elements; how exact they have to be, the bound alone decides.
A program may use at most 192 MiB of HBM per device.

v0:
```python
import math
import jax
import jax.numpy as jnp
from jax import lax
from jax.sharding import PartitionSpec as P

HEAD_DIM = 160
EPS = 1e-05
NEG = -1e30


def layer_norm(v, gain, shift):
    center = v - jnp.mean(v, axis=-1, keepdims=True)
    spread = jnp.mean(center * center, axis=-1, keepdims=True)
    return center * lax.rsqrt(spread + EPS) * gain + shift


def inner(left, right):
    return lax.dot_general(
        left, right, (((0,), (0,)), ((), ())), preferred_element_type=jnp.float32
    )


def outer(left, right):
    return lax.dot_general(
        left, right, (((1,), (1,)), ((), ())), preferred_element_type=jnp.float32
    )


def mask_of(seg):
    length = seg.shape[0]
    rowpos = lax.broadcasted_iota(jnp.int32, (length, length), 0)
    colpos = lax.broadcasted_iota(jnp.int32, (length, length), 1)
    return ((rowpos >= colpos) & (seg[:, None] == seg[None, :]))[None]


def scores_of(query, keyed, seg):
    scores = jnp.einsum(
        "qhe,khe->hqk", query, keyed, preferred_element_type=jnp.float32
    ) / math.sqrt(HEAD_DIM)
    allowed = mask_of(seg)
    return (jnp.where(allowed, scores, NEG), allowed)


def attend_forward(query, keyed, valued, seg):
    scores, allowed = scores_of(query, keyed, seg)
    top = jnp.max(scores, axis=-1, keepdims=True)
    weights = jnp.where(allowed, jnp.exp(scores - top), 0.0)
    total = jnp.sum(weights, axis=-1, keepdims=True)
    probs = (weights / total).astype(jnp.bfloat16)
    mixed = jnp.einsum("hqk,khe->qhe", probs, valued, preferred_element_type=jnp.float32).astype(
        jnp.bfloat16
    )
    return (mixed, (top + jnp.log(total))[..., 0])


def attend_backward(query, keyed, valued, seg, logsum, d_mixed):
    scores, allowed = scores_of(query, keyed, seg)
    probs = jnp.where(allowed, jnp.exp(scores - logsum[..., None]), 0.0)
    low_probs = probs.astype(jnp.bfloat16)
    d_valued = jnp.einsum(
        "hqk,qhe->khe", low_probs, d_mixed, preferred_element_type=jnp.float32
    ).astype(jnp.bfloat16)
    d_probs = jnp.einsum("qhe,khe->hqk", d_mixed, valued, preferred_element_type=jnp.float32)
    d_scores = probs * (d_probs - jnp.sum(probs * d_probs, axis=-1, keepdims=True))
    low_scores = d_scores.astype(jnp.bfloat16)
    scale = 1.0 / math.sqrt(HEAD_DIM)
    d_query = (
        jnp.einsum("hqk,khe->qhe", low_scores, keyed, preferred_element_type=jnp.float32) * scale
    ).astype(jnp.bfloat16)
    d_keyed = (
        jnp.einsum("hqk,qhe->khe", low_scores, query, preferred_element_type=jnp.float32) * scale
    ).astype(jnp.bfloat16)
    return (d_query, d_keyed, d_valued)


def shards(
    latents,
    norm1_gain,
    norm1_shift,
    query_weight,
    query_bias,
    key_weight,
    value_weight,
    value_bias,
    out_weight,
    out_bias,
    norm2_gain,
    norm2_shift,
    hidden_weight,
    hidden_bias,
    proj_weight,
    proj_bias,
    segments,
    valid_mask,
    cotangent,
):
    seq_count, length = segments.shape
    tok_rows, width = latents.shape
    local_heads = query_weight.shape[1] // HEAD_DIM

    def split(t):
        return t.reshape(seq_count, length, local_heads, HEAD_DIM)

    inputs = latents.astype(jnp.float32)
    normed1 = layer_norm(inputs, norm1_gain, norm1_shift).astype(jnp.bfloat16)
    query = (
        jnp.dot(normed1, query_weight, preferred_element_type=jnp.float32) + query_bias
    ).astype(jnp.bfloat16)
    keyed = jnp.dot(normed1, key_weight, preferred_element_type=jnp.float32).astype(jnp.bfloat16)
    valued = (
        jnp.dot(normed1, value_weight, preferred_element_type=jnp.float32) + value_bias
    ).astype(jnp.bfloat16)
    mixed, logsum = lax.map(
        lambda t: attend_forward(t[0], t[1], t[2], t[3]),
        (split(query), split(keyed), split(valued), segments),
    )
    mixed = mixed.reshape(tok_rows, local_heads * HEAD_DIM)
    attended = (
        lax.psum(jnp.dot(mixed, out_weight, preferred_element_type=jnp.float32), "tensor")
        + out_bias
    )
    resid = inputs + attended
    normed2 = layer_norm(resid, norm2_gain, norm2_shift).astype(jnp.bfloat16)
    pre = jnp.dot(normed2, hidden_weight, preferred_element_type=jnp.float32) + hidden_bias
    act = jax.nn.gelu(pre, approximate=False).astype(jnp.bfloat16)
    branch = (
        lax.psum(jnp.dot(act, proj_weight, preferred_element_type=jnp.float32), "tensor")
        + proj_bias
    )
    output = resid + branch
    weight = valid_mask.astype(jnp.float32)
    counted = jnp.maximum(jnp.sum(weight, axis=1), 1.0) * width

    def per_seq(v):
        return jnp.sum(weight * jnp.sum(v * v, axis=-1).reshape(seq_count, length), axis=1)

    stat_sums = jnp.stack([per_seq(attended), per_seq(branch), per_seq(output)], axis=1)
    rms = jnp.sqrt(stat_sums / counted[:, None])
    grad_out = cotangent.astype(jnp.float32)
    grad_w2 = inner(act, cotangent)
    grad_b2 = jnp.sum(grad_out, axis=0)
    d_act = outer(cotangent, proj_weight)
    d_pre = jax.vjp(lambda t: jax.nn.gelu(t, approximate=False), pre)[1](d_act)[0]
    low_pre = d_pre.astype(jnp.bfloat16)
    grad_w1 = inner(normed2, low_pre)
    grad_b1 = jnp.sum(low_pre.astype(jnp.float32), axis=0)
    d_normed2 = lax.psum(outer(low_pre, hidden_weight), "tensor")
    norm_back2 = jax.vjp(layer_norm, resid, norm2_gain, norm2_shift)[1]
    d_resid_norm, grad_g2, grad_c2 = norm_back2(d_normed2)
    d_resid = grad_out + d_resid_norm
    low_attended = d_resid.astype(jnp.bfloat16)
    grad_bo = jnp.sum(low_attended.astype(jnp.float32), axis=0)
    grad_wo = inner(mixed, low_attended)
    d_mixed = outer(low_attended, out_weight).astype(jnp.bfloat16)
    d_query, d_keyed, d_valued = lax.map(
        lambda t: attend_backward(t[0], t[1], t[2], t[3], t[4], t[5]),
        (split(query), split(keyed), split(valued), segments, logsum, split(d_mixed)),
    )
    d_query = d_query.reshape(tok_rows, local_heads * HEAD_DIM)
    d_keyed = d_keyed.reshape(tok_rows, local_heads * HEAD_DIM)
    d_valued = d_valued.reshape(tok_rows, local_heads * HEAD_DIM)
    grad_wq = inner(normed1, d_query)
    grad_bq = jnp.sum(d_query.astype(jnp.float32), axis=0)
    grad_wk = inner(normed1, d_keyed)
    grad_wv = inner(normed1, d_valued)
    grad_bv = jnp.sum(d_valued.astype(jnp.float32), axis=0)
    partial_in = (
        outer(d_query, query_weight) + outer(d_keyed, key_weight) + outer(d_valued, value_weight)
    )
    d_normed1 = lax.psum(partial_in, "tensor")
    norm_back1 = jax.vjp(layer_norm, inputs, norm1_gain, norm1_shift)[1]
    d_input_norm, grad_g1, grad_c1 = norm_back1(d_normed1)
    grad_input = d_resid + d_input_norm
    (
        grad_g1,
        grad_c1,
        grad_wq,
        grad_bq,
        grad_wk,
        grad_wv,
        grad_bv,
        grad_wo,
        grad_bo,
        grad_g2,
        grad_c2,
        grad_w1,
        grad_b1,
        grad_w2,
        grad_b2,
    ) = lax.psum(
        (
            grad_g1,
            grad_c1,
            grad_wq,
            grad_bq,
            grad_wk,
            grad_wv,
            grad_bv,
            grad_wo,
            grad_bo,
            grad_g2,
            grad_c2,
            grad_w1,
            grad_b1,
            grad_w2,
            grad_b2,
        ),
        "dp",
    )
    return (
        output.astype(jnp.bfloat16),
        grad_input,
        grad_g1,
        grad_c1,
        grad_wq,
        grad_bq,
        grad_wk,
        grad_wv,
        grad_bv,
        grad_wo,
        grad_bo,
        grad_g2,
        grad_c2,
        grad_w1,
        grad_b1,
        grad_w2,
        grad_b2,
        rms,
    )


def solution(mesh):
    placed = (
        P("dp", None),
        P(),
        P(),
        P(None, "tensor"),
        P("tensor"),
        P(None, "tensor"),
        P(None, "tensor"),
        P("tensor"),
        P("tensor", None),
        P(),
        P(),
        P(),
        P(None, "tensor"),
        P("tensor"),
        P("tensor", None),
        P(),
        P("dp", None),
        P("dp", None),
        P("dp", None),
    )
    return jax.shard_map(
        shards,
        mesh=mesh,
        in_specs=placed,
        out_specs=(
            P("dp", None),
            P("dp", None),
            P(),
            P(),
            P(None, "tensor"),
            P("tensor"),
            P(None, "tensor"),
            P(None, "tensor"),
            P("tensor"),
            P("tensor", None),
            P(),
            P(),
            P(),
            P(None, "tensor"),
            P("tensor"),
            P("tensor", None),
            P(),
            P("dp", None),
        ),
        check_vma=False,
    )
```

profile of v0, /device:TPU:0, one launch (start us, length us, event | category | flops | bytes accessed | tf_op | source)
XLA Modules:
  0.0 1821.8 jit_solution(10788580656488504458)
XLA Ops:
  7.3 3.4 convert_reduce_fusion
  13.0 2.4 fusion.64
  21.8 5.4 fusion.71
  27.3 3.6 reshape.252
  32.3 4.4 fusion.70
  41.4 20.8 %while.26 = (s32[]{:T(128)}, bf16[2,1024,2,160]{1,3,2,0:T(8,128)(2,1)}, f32[2,2,1024]{2,1,0:T(2,128)S(1)}, bf16[2,1024,2,160]{1,3,2,0:T(8,128)(2,1)S(1)}, s32[2,...) while((s32[]{:T(128)}, ...), condition=%wide.region_5.6_spmd, body=%wide.region_2.5_spmd.sunk | while | flops 1375008768 | bytes 42547356 | solution.py:114
  42.3 3.1 fusion.156
  47.7 3.2 fusion.158
  52.5 3.1 fusion.156
  57.9 3.2 fusion.158
  62.2 3.6 copy.56
  67.3 5.7 fusion.87
  73.5 360.7 %all-reduce.8.cloned.1.call-done = f32[2048,1280]{1,0:T(8,128)} async-done(((f32[2048,1280]{1,0:T(8,128)}), f32[2048,1280]{1,0:T(8,128)}) %all-reduce.8.cloned.1.call-update) | async-done | bytes 10485776 | tf_op jit(solution)/shard_map/psum | solution.py:120
  434.3 11.8 fusion.86
  446.1 5.3 multiply_reduce_fusion.6
  459.3 10.2 convert_reduce_fusion.3
  470.1 5.5 fusion.88
  475.6 5.4 fusion.89
  481.3 697.6 %all-reduce.14.cloned.1.call-done = (f32[2048,1280]{1,0:T(8,128)}, f32[2048,1280]{1,0:T(8,128)}) async-done(((f32[2048,1280]{1,0:T(8,128)}, f32[2048,1280]{1,0:T(8,128)}), (f32[2048,1280]{1,0:T(8,128)}, f32[2048,1280]{1,0:T(8,128)})) %all-reduce.14.cloned.1.call-update) | async-done | bytes 20971536 | tf_op jit(solution)/shard_map/psum | solution.py:128
  1179.0 15.7 multiply_reduce_fusion.2
  1196.9 3.9 fusion.85
  1200.9 7.7 convert_reduce_fusion.2
  1220.0 55.4 %while.27 = (s32[]{:T(128)}, bf16[2,1024,2,160]{1,3,2,0:T(8,128)(2,1)}, bf16[2,1024,2,160]{1,3,2,0:T(8,128)(2,1)}, bf16[2,1024,2,160]{1,3,2,0:T(8,128)(2,1)}, bf...) while((s32[]{:T(128)}, ...), condition=%wide.region_15.16_spmd, body=%wide.region_13.15_spmd.sunk | while | flops 3381196800 | bytes 147121552 | solution.py:156
  1220.9 2.6 fusion.167
  1223.5 6.0 multiply_reduce_fusion.11
  1229.6 8.2 multiply_convert_fusion.3
  1237.8 6.0 fusion.171
  1248.3 2.6 fusion.167
  1250.9 6.0 multiply_reduce_fusion.11
  1257.0 8.2 multiply_convert_fusion.3
  1265.2 6.0 fusion.171
  1275.4 2.8 copy.62
  1283.1 3.0 fusion.91
  1286.1 3.0 fusion.90
  1289.1 9.0 add_add_fusion.3
  1299.5 5.7 fusion.97
  1305.2 3.1 fusion.93
  1308.5 5.7 fusion.92
  1314.2 5.7 fusion.96
  1319.9 3.0 fusion.94
  1323.0 3.0 fusion.95
  1328.3 327.4 %all-reduce.10.cloned.1.call-done = f32[2048,1280]{1,0:T(8,128)} async-done(((f32[2048,1280]{1,0:T(8,128)}), f32[2048,1280]{1,0:T(8,128)}) %all-reduce.10.cloned.1.call-update) | async-done | bytes 10485776 | tf_op jit(solution)/shard_map/psum | solution.py:171
  1655.7 7.9 fusion.82
  1663.7 9.8 fusion.65
  1673.7 12.9 convert_reduce_fusion.1
  1686.5 26.9 %all-reduce = (f32[1280]{0:T(1024)}, f32[1280]{0:T(1024)}, f32[320]{0:T(512)}, f32[320]{0:T(512)}, f32[1280]{0:T(1024)}, /*index=5*/f32[1280]{0:T(1024)}, f32[1280]{0:T(1024)}, f32[320]{0:T(512)}, f32[1280]{0:T(1024)}) all-reduce(f32[1280]{0:T(1024)S(1)} %get-tuple-element.187, ...), channel_id=1, replica_groups=mesh['dp'=8,'tensor'=4] {'dp'}, use_global_device_ids=true, to_apply=%region_20.21 | all-reduce | flops 8640 | bytes 69120 | tf_op jit(solution)/shard_map/psum | solution.py:191
  1713.5 92.8 %all-reduce.12.cloned.1.call-done = (f32[1280,320]{0,1:T(8,128)}, f32[1280,320]{0,1:T(8,128)}, f32[1280,320]{0,1:T(8,128)}, f32[320,1280]{1,0:T(8,128)}, f32[1280,320]{0,1:T(8,128)}, /*index=5*/f32[320,1280]{1,0:T(8,128)}) async-done(((f32[1280,320]{0,1:T(8,128)}, f32[1280,320]{0,1:T(8,128)}, f32[1280,320]{0,1:T(8,128)}, f32[320,1280]{1,0:T(8,128)}, f32[1280,320]{0,1:T(8,128)}, ...) | async-done | bytes 9830416 | tf_op jit(solution)/shard_map/psum | solution.py:191
  1806.3 2.8 copy.111
  (290 shorter events, 70.6 us)
Async XLA Ops:
  7.2 450.7 %copy-start = (bf16[320,1280]{1,0:T(8,128)(2,1)S(1)}, bf16[320,1280]{1,0:T(8,128)(2,1)}, u32[]{:S(2)}) copy-start(bf16[320,1280]{1,0:T(8,128)(2,1)} %param.37) | copy-start | bytes 2457604
  7.2 427.1 %all-reduce.8.cloned.1.call-start = ((), (), s32[]{:S(2)}) async-start(), calls=%async_computation | async-start | bytes 20971520 | tf_op jit(solution)/shard_map/psum | solution.py:120
  72.9 361.3 %copy-start.69 = (f32[1280]{0:T(1024)S(1)}, f32[1280]{0:T(1024)}, u32[]{:S(2)}) copy-start(f32[1280]{0:T(1024)} %param.32) | copy-start | bytes 15364
  73.0 1106.0 %all-reduce.14.cloned.1.call-start = ((), (), s32[]{:S(2)}) async-start(), calls=%async_computation.3 | async-start | bytes 41943040 | tf_op jit(solution)/shard_map/psum | solution.py:128
  446.1 7.0 copy-start.3
  446.1 7.0 copy-start.57
  446.1 7.0 copy-start.70
  469.5 6.1 copy-start.34
  481.0 697.9 %copy-start.71 = (f32[1280]{0:T(1024)S(1)}, f32[1280]{0:T(1024)}, u32[]{:S(2)}) copy-start(f32[1280]{0:T(1024)} %param.38) | copy-start | bytes 15364
  481.1 1174.7 %all-reduce.10.cloned.1.call-start = ((), (), s32[]{:S(2)}) async-start(), calls=%async_computation.1 | async-start | bytes 20971520 | tf_op jit(solution)/shard_map/psum | solution.py:171
  1178.9 15.8 slice-start
  1178.9 15.8 slice-start.8
  1178.9 15.8 slice-start.1
  1178.9 16.2 slice-start.2
  1179.0 17.4 slice-start.9
  1179.0 18.0 slice-start.10
  1200.8 7.8 copy-start.5
  1200.8 7.8 copy-start.58
  1200.8 10.1 copy-start.45
  1223.5 6.0 copy-start.2
  1237.8 6.0 copy-start.11
  1237.8 6.0 copy-start.28
  1250.9 6.0 copy-start.2
  1265.2 6.0 copy-start.11
  1265.2 6.0 copy-start.28
  1280.3 5.8 copy-start.22
  1298.2 7.0 slice-start.13
  1298.2 508.1 %all-reduce.12.cloned.1.call-start = ((), (), s32[]{:S(2)}) async-start(), calls=%async_computation.2 | async-start | bytes 19660800 | tf_op jit(solution)/shard_map/psum | solution.py:191
  1299.5 5.7 slice-start.14
  1299.5 5.7 copy-start.25
  1308.5 5.7 copy-start.26
  1308.5 11.4 slice-start.15
  1314.2 5.7 copy-start.23
  1314.2 5.7 slice-start.16
  1326.0 329.7 %copy-start.51 = (f32[2048]{0:T(1024)S(1)}, f32[2048]{0:T(1024)}, u32[]{:S(2)}) copy-start(f32[2048]{0:T(1024)} %copy-done.50) | copy-start | bytes 24580
  1326.0 329.7 %copy-start.54 = (f32[1280]{0:T(1024)S(1)}, f32[1280]{0:T(1024)}, u32[]{:S(2)}) copy-start(f32[1280]{0:T(1024)} %param.24) | copy-start | bytes 15364
  1328.3 335.3 %copy-start.61 = (f32[2048]{0:T(1024)S(1)}, f32[2048]{0:T(1024)}, u32[]{:S(2)}) copy-start(f32[2048]{0:T(1024)} %copy-done.60) | copy-start | bytes 24580
  1328.3 335.4 %copy-start.56 = (f32[2048]{0:T(1024)S(1)}, f32[2048]{0:T(1024)}, u32[]{:S(2)}) copy-start(f32[2048]{0:T(1024)} %copy-done.55) | copy-start | bytes 24580
  1655.7 17.8 slice-start.5
  1655.7 17.8 slice-start.6
  1663.7 9.9 slice-start.3
  1663.7 9.9 slice-start.4
  1663.7 9.9 slice-start.7
  1663.7 9.9 copy-start.59
  1673.6 12.9 copy-start.62
  1673.6 12.9 copy-start.63
  1673.6 12.9 copy-start.64
  1673.7 12.9 copy-start.73
  (61 other events, 155.3 us)
Sparse Core Ops, SparseCore 0:
  73.1 361.1 all-reduce.7
  481.2 697.6 all-reduce.13
  1298.3 357.3 all-reduce.9
  1662.1 144.1 all-reduce.11
where the time goes:
time: 1830 us; the launch traced here: 1820 us
  waiting for transfers between devices  1480 us (81%)
  matrix products  130 us (7%)
  other arithmetic  109 us (6%)
  local copies, waits for them, and re-layouts  60.1 us (3%)
  blocking collectives  26.9 us (1%)
    psum x1, waiting for transfers between devices, shards(): lax.psum(jnp.dot(act, proj_weight, preferred_element_type=jnp.float32), '...  698 us
    psum x1, waiting for transfers between devices, shards(): lax.psum(jnp.dot(mixed, out_weight, preferred_element_type=jnp.float32),...  361 us
    psum x1, waiting for transfers between devices, shards(): d_normed1 = lax.psum(partial_in, 'tensor')  327 us
    psum x1, waiting for transfers between devices, shards(): lax.psum((grad_g1, grad_c1, grad_wq, grad_bq, grad_wk, grad_wv, grad_bv,...  92.8 us
  transfers between devices with their start and end apart: 4, of which 4 were waited for; matrix products, arithmetic and copies ran while one was open for 3% of the time, Pallas kernels for 0%

commit v1 on v0

--- a/solution.py
+++ b/solution.py
@@ -117,7 +117,12 @@
     )
     mixed = mixed.reshape(tok_rows, local_heads * HEAD_DIM)
     attended = (
-        lax.psum(jnp.dot(mixed, out_weight, preferred_element_type=jnp.float32), "tensor")
+        jnp.sum(
+            lax.all_gather(
+                jnp.dot(mixed, out_weight, preferred_element_type=jnp.float32), "tensor"
+            ),
+            axis=0,
+        )
         + out_bias
     )
     resid = inputs + attended

time: 1830 us -> 2190 us (1.20)
  waiting for transfers between devices: 1480 us -> 1820 us
    all_gather x0 -> x1, waiting for transfers between devices: none -> 703 us  [shards(): lax.all_gather(jnp.dot(mixed, out_weight, preferred_element_type=jnp.floa...]
    psum x1 -> x0, waiting for transfers between devices: 361 us -> none  [shards(): lax.psum(jnp.dot(mixed, out_weight, preferred_element_type=jnp.float32),...]
where the time goes in v1:
time: 2190 us; the launch traced here: 2180 us
  waiting for transfers between devices  1820 us (83%)
  other arithmetic  130 us (6%)
  matrix products  130 us (6%)
  local copies, waits for them, and re-layouts  59.8 us (3%)
  blocking collectives  26.9 us (1%)
    all_gather x1, waiting for transfers between devices, shards(): lax.all_gather(jnp.dot(mixed, out_weight, preferred_element_type=jnp.floa...  703 us
    psum x1, waiting for transfers between devices, shards(): lax.psum(jnp.dot(act, proj_weight, preferred_element_type=jnp.float32), '...  697 us
    psum x1, waiting for transfers between devices, shards(): d_normed1 = lax.psum(partial_in, 'tensor')  327 us
    psum x1, waiting for transfers between devices, shards(): lax.psum((grad_g1, grad_c1, grad_wq, grad_bq, grad_wk, grad_wv, grad_bv,...  92.8 us
  transfers between devices with their start and end apart: 4, of which 4 were waited for; matrix products, arithmetic and copies ran while one was open for 3% of the time, Pallas kernels for 0%

profile of v1, /device:TPU:0, one launch (start us, length us, event | category | flops | bytes accessed | tf_op | source)
XLA Modules:
  0.0 2182.7 jit_solution(1729148789519911559)
XLA Ops:
  7.3 3.4 convert_reduce_fusion
  21.8 5.4 fusion.71
  27.3 3.6 reshape.252
  32.3 4.4 fusion.70
  41.4 20.7 while.26
  42.2 3.1 fusion.156
  47.6 3.2 fusion.158
  52.4 3.1 fusion.156
  57.8 3.2 fusion.158
  62.1 3.6 copy.56
  67.2 5.7 fusion.87
  72.9 702.6 %all-gather.3.cloned.1.call-done = f32[8192,1280]{1,0:T(8,128)} async-done(((f32[2048,1280]{1,0:T(8,128)}), f32[8192,1280]{1,0:T(8,128)}) %all-gather.3.cloned.1.call-update) | async-done | bytes 41943056 | tf_op jit(solution)/shard_map/all_gather | solution.py:121
  775.5 20.3 reduce_sum.248
  795.8 11.8 fusion.86
  807.6 5.3 multiply_reduce_fusion.6
  820.8 10.2 convert_reduce_fusion.3
  831.6 5.5 fusion.88
  837.1 5.4 fusion.89
  842.6 697.0 %all-reduce.11.cloned.1.call-done = (f32[2048,1280]{1,0:T(8,128)}, f32[2048,1280]{1,0:T(8,128)}) async-done(((f32[2048,1280]{1,0:T(8,128)}, f32[2048,1280]{1,0:T(8,128)}), (f32[2048,1280]{1,0:T(8,128)}, f32[2048,1280]{1,0:T(8,128)})) %all-reduce.11.cloned.1.call-update) | async-done | bytes 20971536 | tf_op jit(solution)/shard_map/psum | solution.py:133
  1539.7 15.9 multiply_reduce_fusion.2
  1557.6 3.9 fusion.85
  1561.5 7.7 convert_reduce_fusion.2
  1580.7 55.4 %while.27 = (s32[]{:T(128)}, bf16[2,1024,2,160]{1,3,2,0:T(8,128)(2,1)}, bf16[2,1024,2,160]{1,3,2,0:T(8,128)(2,1)}, bf16[2,1024,2,160]{1,3,2,0:T(8,128)(2,1)}, bf...) while((s32[]{:T(128)}, ...), condition=%wide.region_15.16_spmd, body=%wide.region_13.15_spmd.sunk | while | flops 3381196800 | bytes 147121552 | solution.py:161
  1581.8 2.6 fusion.167
  1584.5 6.0 multiply_reduce_fusion.11
  1590.5 8.2 multiply_convert_fusion.3
  1598.8 6.0 fusion.171
  1609.2 2.6 fusion.167
  1611.9 6.0 multiply_reduce_fusion.11
  1617.9 8.2 multiply_convert_fusion.3
  1626.2 6.0 fusion.171
  1636.1 2.8 copy.62
  1643.9 3.0 fusion.91
  1646.9 3.0 fusion.90
  1649.8 9.1 add_add_fusion.3
  1660.2 5.7 fusion.97
  1666.0 3.1 fusion.93
  1669.3 5.7 fusion.92
  1674.9 5.7 fusion.96
  1680.7 3.0 fusion.94
  1683.7 3.0 fusion.95
  1689.1 327.4 %all-reduce.7.cloned.1.call-done = f32[2048,1280]{1,0:T(8,128)} async-done(((f32[2048,1280]{1,0:T(8,128)}), f32[2048,1280]{1,0:T(8,128)}) %all-reduce.7.cloned.1.call-update) | async-done | bytes 10485776 | tf_op jit(solution)/shard_map/psum | solution.py:176
  2016.5 7.9 fusion.82
  2024.5 9.8 fusion.65
  2034.5 12.9 convert_reduce_fusion.1
  2047.4 26.9 %all-reduce = (f32[1280]{0:T(1024)}, f32[1280]{0:T(1024)}, f32[320]{0:T(512)}, f32[320]{0:T(512)}, f32[1280]{0:T(1024)}, /*index=5*/f32[1280]{0:T(1024)}, f32[1280]{0:T(1024)}, f32[320]{0:T(512)}, f32[1280]{0:T(1024)}) all-reduce(f32[1280]{0:T(1024)S(1)} %get-tuple-element.187, ...), channel_id=1, replica_groups=mesh['dp'=8,'tensor'=4] {'dp'}, use_global_device_ids=true, to_apply=%region_20.21 | all-reduce | flops 8640 | bytes 69120 | tf_op jit(solution)/shard_map/psum | solution.py:196
  2074.2 92.8 %all-reduce.9.cloned.1.call-done = (f32[1280,320]{0,1:T(8,128)}, f32[1280,320]{0,1:T(8,128)}, f32[1280,320]{0,1:T(8,128)}, f32[320,1280]{1,0:T(8,128)}, f32[1280,320]{0,1:T(8,128)}, /*index=5*/f32[320,1280]{1,0:T(8,128)}) async-done(((f32[1280,320]{0,1:T(8,128)}, f32[1280,320]{0,1:T(8,128)}, f32[1280,320]{0,1:T(8,128)}, f32[320,1280]{1,0:T(8,128)}, f32[1280,320]{0,1:T(8,128)}, ...) | async-done | bytes 9830416 | tf_op jit(solution)/shard_map/psum | solution.py:196
  2167.1 2.8 copy.110
  (291 shorter events, 72.0 us)
Async XLA Ops:
  7.2 812.2 %copy-start = (bf16[320,1280]{1,0:T(8,128)(2,1)S(1)}, bf16[320,1280]{1,0:T(8,128)(2,1)}, u32[]{:S(2)}) copy-start(bf16[320,1280]{1,0:T(8,128)(2,1)} %param.37) | copy-start | bytes 2457604
  7.2 768.3 %all-gather.3.cloned.1.call-start = ((), (), s32[]{:S(2)}) async-start(), calls=%async_computation.1 | async-start | bytes 52428800 | tf_op jit(solution)/shard_map/all_gather | solution.py:121
  72.8 1466.8 %all-reduce.11.cloned.1.call-start = ((), (), s32[]{:S(2)}) async-start(), calls=%async_computation.3 | async-start | bytes 41943040 | tf_op jit(solution)/shard_map/psum | solution.py:133
  775.5 20.3 copy-start.69
  807.6 7.0 copy-start.3
  807.6 7.0 copy-start.57
  807.6 7.0 copy-start.70
  831.0 6.1 copy-start.34
  842.6 697.1 %copy-start.71 = (f32[1280]{0:T(1024)S(1)}, f32[1280]{0:T(1024)}, u32[]{:S(2)}) copy-start(f32[1280]{0:T(1024)} %param.38) | copy-start | bytes 15364
  842.6 1173.9 %all-reduce.7.cloned.1.call-start = ((), (), s32[]{:S(2)}) async-start(), calls=%async_computation | async-start | bytes 20971520 | tf_op jit(solution)/shard_map/psum | solution.py:176
  1539.6 16.0 slice-start
  1539.6 16.0 slice-start.8
  1539.6 16.0 slice-start.1
  1539.6 16.2 slice-start.2
  1539.7 17.4 slice-start.9
  1539.7 18.0 slice-start.10
  1561.5 7.8 copy-start.5
  1561.5 7.8 copy-start.58
  1561.5 10.1 copy-start.45
  1584.5 6.0 copy-start.2
  1598.8 6.0 copy-start.11
  1598.8 6.0 copy-start.28
  1611.9 6.0 copy-start.2
  1626.2 6.0 copy-start.11
  1626.2 6.0 copy-start.28
  1641.0 5.8 copy-start.22
  1658.9 7.0 slice-start.13
  1658.9 508.1 %all-reduce.9.cloned.1.call-start = ((), (), s32[]{:S(2)}) async-start(), calls=%async_computation.2 | async-start | bytes 19660800 | tf_op jit(solution)/shard_map/psum | solution.py:196
  1660.2 5.7 slice-start.14
  1660.2 5.7 copy-start.25
  1669.2 5.7 copy-start.26
  1669.3 11.4 slice-start.15
  1674.9 5.7 copy-start.23
  1674.9 5.7 slice-start.16
  1686.8 329.7 %copy-start.51 = (f32[2048]{0:T(1024)S(1)}, f32[2048]{0:T(1024)}, u32[]{:S(2)}) copy-start(f32[2048]{0:T(1024)} %copy-done.50) | copy-start | bytes 24580
  1686.8 329.7 %copy-start.54 = (f32[1280]{0:T(1024)S(1)}, f32[1280]{0:T(1024)}, u32[]{:S(2)}) copy-start(f32[1280]{0:T(1024)} %param.24) | copy-start | bytes 15364
  1689.1 335.3 %copy-start.61 = (f32[2048]{0:T(1024)S(1)}, f32[2048]{0:T(1024)}, u32[]{:S(2)}) copy-start(f32[2048]{0:T(1024)} %copy-done.60) | copy-start | bytes 24580
  1689.1 335.4 %copy-start.56 = (f32[2048]{0:T(1024)S(1)}, f32[2048]{0:T(1024)}, u32[]{:S(2)}) copy-start(f32[2048]{0:T(1024)} %copy-done.55) | copy-start | bytes 24580
  2016.5 17.9 slice-start.5
  2016.5 17.9 slice-start.6
  2024.4 9.9 slice-start.3
  2024.5 9.9 slice-start.4
  2024.5 9.9 slice-start.7
  2024.5 9.9 copy-start.59
  2034.4 12.9 copy-start.62
  2034.4 12.9 copy-start.63
  2034.4 12.9 copy-start.64
  2034.5 12.9 copy-start.73
  (61 other events, 155.3 us)
Sparse Core Ops, SparseCore 0:
  73.0 702.4 all-gather.2
  842.7 696.8 all-reduce.10
  1659.1 357.3 all-reduce.6
  2022.8 144.1 all-reduce.8
